TPU v7x, 256 devices: a whole 4x4x8 slice. The times are simulated.
256 devices in a mesh: section: 32 (over y_hi, z, core), dp: 8 (over y_lo, x).
Axes of the slice: x: 4, y: 4 (y_hi: 2, y_lo: 2; y = y_hi * 2 + y_lo), z: 8, core: 2. Of those that a mesh axis runs over, the one named last changes fastest.
Arguments:
- inputs: bfloat16 [8, 128, 4096], P(None, 'dp'), may hold values from -30 to 30
- in_blocks: bfloat16 [2, 32, 112, 1, 128, 128], P(None, 'section', 'dp'), may hold values from -0.5 to 0.5
- in_ids: int32 [2, 32, 112, 1], P(None, 'section', 'dp'), may hold values from 0 to 31, as said below
- out_blocks: bfloat16 [2, 32, 32, 8, 128, 128], P(None, 'section', 'dp'), may hold values from -0.09375 to 0.09375
- out_ids: int32 [2, 32, 32, 8], P(None, 'section', 'dp'), may hold values from 0 to 111, as said below
Outputs:
- activations: bfloat16 [2, 32, 8, 128, 4096], P(None, 'section', None, 'dp')
Inputs may be any that keep to these rules, and one draw needn't show every extreme that they name: `in_ids`: for every layer and every block column, the 1 block rows are distinct. `out_ids`: for every layer and every block column, the 8 block rows are distinct.
All inputs are finite; a program needn't handle non-finite values.
Results may differ from a plain program's by a relative error of at most 0.039.
Values may be sent and summed in bfloat16 or wider, within the bound.
A program may use at most 128 MiB of HBM per device.

v0:
```python
import jax
import jax.numpy as jnp
from jax import lax
from jax.sharding import PartitionSpec as P


def shifted(array, axis, by):
    size = lax.axis_size(axis)
    return lax.ppermute(array, axis, [(i, (i + by) % size) for i in range(size)])


def select_blocks(blocks, block_ids):
    row_count, block_count, block_size = blocks.shape
    picked = jnp.take(blocks, block_ids.reshape(-1), axis=1)
    return picked.reshape(row_count, block_ids.shape[0], block_ids.shape[1], block_size)


def apply_layer(params, incoming):
    proj_weight, proj_ids, back_weight, back_ids = params
    row_count, feat_count = incoming.shape
    block_size = proj_weight.shape[-1]
    values = incoming.astype(jnp.float32)
    inv_root = lax.rsqrt(jnp.mean(values * values, axis=-1, keepdims=True) + 1e-05)
    normed = (values * inv_root).astype(jnp.bfloat16)
    blocks = normed.reshape(row_count, feat_count // block_size, block_size)
    picked = select_blocks(blocks, proj_ids)
    projected = jnp.einsum(
        "rjkc,jkcd->rjd", picked, proj_weight, preferred_element_type=jnp.float32
    )
    hidden = jax.nn.silu(projected).astype(jnp.bfloat16)
    second = select_blocks(hidden, back_ids)
    returned = jnp.einsum("rjkc,jkcd->rjd", second, back_weight, preferred_element_type=jnp.float32)
    return (values + returned.reshape(row_count, feat_count)).astype(jnp.bfloat16)


def lap_params(gathered, lap_index):
    return tuple((array[lap_index, 0] for array in gathered))


def shards(inputs, in_blocks, in_ids, out_blocks, out_ids):
    section_count = lax.axis_size("section")
    my_section = lax.axis_index("section")
    piece_count, row_count, feat_count = inputs.shape
    tick_count = 2 * section_count + piece_count - 1

    def run_tick(tick_num, state_pair, params):
        incoming, stored = state_pair
        offset = tick_num - my_section
        lap_zero = (offset >= 0) & (offset < piece_count)
        lap_one = (offset >= section_count) & (offset < section_count + piece_count)
        piece_num = jnp.clip(jnp.where(lap_one, offset - section_count, offset), 0, piece_count - 1)
        lap_num = jnp.where(lap_one, 1, 0).astype(jnp.int32)
        fresh_rows = lax.dynamic_index_in_dim(inputs, piece_num, 0, keepdims=False)
        source = jnp.where((my_section == 0) & lap_zero, fresh_rows, incoming)

        def work_tick(stored_now):

            def use_second(rows_in):
                return apply_layer(params[1], rows_in)

            def use_first(rows_in):
                return apply_layer(params[0], rows_in)

            result = lax.cond(lap_one, use_second, use_first, source)
            zero_index = jnp.zeros((), jnp.int32)
            updated = lax.dynamic_update_slice(
                stored_now, result[None, None], (lap_num, piece_num, zero_index, zero_index)
            )
            return (updated, result)

        def skip_tick(stored_now):
            return (stored_now, jnp.zeros_like(source))

        stored, result = lax.cond(lap_zero | lap_one, work_tick, skip_tick, stored)
        passed = shifted(result, "section", 1)
        return (passed, stored)

    start_state = (
        jnp.zeros((row_count, feat_count), jnp.bfloat16),
        jnp.zeros((2, piece_count, row_count, feat_count), jnp.bfloat16),
    )
    gathered = (
        lax.all_gather(in_blocks, "dp", axis=2, tiled=True),
        lax.all_gather(in_ids, "dp", axis=2, tiled=True),
        lax.all_gather(out_blocks, "dp", axis=2, tiled=True),
        lax.all_gather(out_ids, "dp", axis=2, tiled=True),
    )
    both_params = (lap_params(gathered, 0), lap_params(gathered, 1))

    def tick_all(tick_num, state_pair):
        return run_tick(tick_num, state_pair, both_params)

    final_state = lax.fori_loop(0, tick_count, tick_all, start_state)
    return final_state[1][:, None]


def solution(mesh):
    return jax.shard_map(
        shards,
        mesh=mesh,
        in_specs=(
            P(None, "dp", None),
            P(None, "section", "dp", None, None, None),
            P(None, "section", "dp", None),
            P(None, "section", "dp", None, None, None),
            P(None, "section", "dp", None),
        ),
        out_specs=P(None, "section", None, "dp", None),
        check_vma=False,
    )
```

profile of v0, /device:TPU:241, one launch (start us, length us, event | category | flops | bytes accessed | tf_op | source)
XLA Modules:
  0.0 1496.6 jit_solution(16947785130232713321)
XLA Ops:
  8.8 23.2 %all_gather.12 = s32[2,1,112,1]{0,3,1,2:T(1,128)S(1)} all-gather(s32[2,1,14,1]{0,3,1,2:T(1,128)S(1)} %copy.20), channel_id=1, replica_groups=mesh['section'=32,'dp'=8] {'dp'}, dimensions={2}, use_global_device_ids=true | all-gather | bytes 1008 | tf_op jit(solution)/shard_map/all_gather | solution.py:84
  33.0 24.3 %all_gather.14 = s32[2,1,32,8]{3,0,1,2:T(2,128)S(1)} all-gather(s32[2,1,4,8]{3,0,1,2:T(2,128)S(1)} %copy.22), channel_id=1, replica_groups=mesh['section'=32,'dp'=8] {'dp'}, dimensions={2}, use_global_device_ids=true | all-gather | bytes 2304 | tf_op jit(solution)/shard_map/all_gather | solution.py:86
  57.3 37.0 %all-gather.3.cloned.1.call-done = bf16[2,1,112,1,128,128]{5,4,2,3,1,0:T(8,128)(2,1)} async-done(((bf16[2,1,14,1,128,128]{5,4,2,3,1,0:T(8,128)(2,1)}), bf16[2,1,112,1,128,128]{5,4,2,3,1,0:T(8,128)(2,1)}) %all-gather.3.cloned.1.call-update) | async-done | bytes 7340048 | tf_op jit(solution)/shard_map/all_gather | solution.py:83
  103.6 164.4 %all-gather.5.cloned.1.call-done = bf16[2,1,32,8,128,128]{5,4,3,2,1,0:T(8,128)(2,1)} async-done(((bf16[2,1,4,8,128,128]{5,4,3,2,1,0:T(8,128)(2,1)}), bf16[2,1,32,8,128,128]{5,4,3,2,1,0:T(8,128)(2,1)}) %all-gather.5.cloned.1.call-update) | async-done | bytes 16777232 | tf_op jit(solution)/shard_map/all_gather | solution.py:85
  281.4 1208.3 %while.20 = (s32[]{:T(128)}, bf16[16,4096]{1,0:T(8,128)(2,1)S(1)}, bf16[2,8,16,4096]{3,2,1,0:T(8,128)(2,1)}, s32[]{:T(128)}, pred[]{:T(512)}, /*index=5*/bf16[8,...) while((s32[]{:T(128)}, bf16[16,4096]{1,0:T(8,128)(2,1)S(1)}, ...), condition=%wide.region_7.10_spmd, body=%wide.region_0.9_spmd.sunk | while | flops 195499280 | bytes 21777136 | solution.py:93
  298.7 19.2 %collective-permute-start = (bf16[16,4096]{1,0:T(8,128)(2,1)}, bf16[16,4096]{1,0:T(8,128)(2,1)S(1)}, u32[]{:S(2)}, u32[]{:S(2)}) collective-permute-start(bf16[16,4096]{1,0:T(8,128)(2,1)} %get-tuple-element.654), channel_id=1, source_target_pairs={{0,8},{8,16},{16,24},{24,32},{32,40},{40,48},{48,56},{56,64},{64,7... | collective-permute-start | bytes 393224 | tf_op jit(solution)/shard_map/while/body/eval_jaxpr/ppermute | solution.py:9
  320.8 19.2 %collective-permute-start = (bf16[16,4096]{1,0:T(8,128)(2,1)}, bf16[16,4096]{1,0:T(8,128)(2,1)S(1)}, u32[]{:S(2)}, u32[]{:S(2)}) collective-permute-start(bf16[16,4096]{1,0:T(8,128)(2,1)} %get-tuple-element.654), channel_id=1, source_target_pairs={{0,8},{8,16},{16,24},{24,32},{32,40},{40,48},{48,56},{56,64},{64,7... | collective-permute-start | bytes 393224 | tf_op jit(solution)/shard_map/while/body/eval_jaxpr/ppermute | solution.py:9
  342.9 19.2 %collective-permute-start = (bf16[16,4096]{1,0:T(8,128)(2,1)}, bf16[16,4096]{1,0:T(8,128)(2,1)S(1)}, u32[]{:S(2)}, u32[]{:S(2)}) collective-permute-start(bf16[16,4096]{1,0:T(8,128)(2,1)} %get-tuple-element.654), channel_id=1, source_target_pairs={{0,8},{8,16},{16,24},{24,32},{32,40},{40,48},{48,56},{56,64},{64,7... | collective-permute-start | bytes 393224 | tf_op jit(solution)/shard_map/while/body/eval_jaxpr/ppermute | solution.py:9
  365.0 19.2 %collective-permute-start = (bf16[16,4096]{1,0:T(8,128)(2,1)}, bf16[16,4096]{1,0:T(8,128)(2,1)S(1)}, u32[]{:S(2)}, u32[]{:S(2)}) collective-permute-start(bf16[16,4096]{1,0:T(8,128)(2,1)} %get-tuple-element.654), channel_id=1, source_target_pairs={{0,8},{8,16},{16,24},{24,32},{32,40},{40,48},{48,56},{56,64},{64,7... | collective-permute-start | bytes 393224 | tf_op jit(solution)/shard_map/while/body/eval_jaxpr/ppermute | solution.py:9
  387.1 19.2 %collective-permute-start = (bf16[16,4096]{1,0:T(8,128)(2,1)}, bf16[16,4096]{1,0:T(8,128)(2,1)S(1)}, u32[]{:S(2)}, u32[]{:S(2)}) collective-permute-start(bf16[16,4096]{1,0:T(8,128)(2,1)} %get-tuple-element.654), channel_id=1, source_target_pairs={{0,8},{8,16},{16,24},{24,32},{32,40},{40,48},{48,56},{56,64},{64,7... | collective-permute-start | bytes 393224 | tf_op jit(solution)/shard_map/while/body/eval_jaxpr/ppermute | solution.py:9
  409.2 19.2 %collective-permute-start = (bf16[16,4096]{1,0:T(8,128)(2,1)}, bf16[16,4096]{1,0:T(8,128)(2,1)S(1)}, u32[]{:S(2)}, u32[]{:S(2)}) collective-permute-start(bf16[16,4096]{1,0:T(8,128)(2,1)} %get-tuple-element.654), channel_id=1, source_target_pairs={{0,8},{8,16},{16,24},{24,32},{32,40},{40,48},{48,56},{56,64},{64,7... | collective-permute-start | bytes 393224 | tf_op jit(solution)/shard_map/while/body/eval_jaxpr/ppermute | solution.py:9
  431.2 19.2 %collective-permute-start = (bf16[16,4096]{1,0:T(8,128)(2,1)}, bf16[16,4096]{1,0:T(8,128)(2,1)S(1)}, u32[]{:S(2)}, u32[]{:S(2)}) collective-permute-start(bf16[16,4096]{1,0:T(8,128)(2,1)} %get-tuple-element.654), channel_id=1, source_target_pairs={{0,8},{8,16},{16,24},{24,32},{32,40},{40,48},{48,56},{56,64},{64,7... | collective-permute-start | bytes 393224 | tf_op jit(solution)/shard_map/while/body/eval_jaxpr/ppermute | solution.py:9
  671.6 117.6 %collective-permute-done = bf16[16,4096]{1,0:T(8,128)(2,1)S(1)} collective-permute-done((bf16[16,4096]{1,0:T(8,128)(2,1)}, bf16[16,4096]{1,0:T(8,128)(2,1)S(1)}, u32[]{:S(2)}, u32[]{:S(2)}) %collective-permute-start) | collective-permute-done | bytes 131104 | tf_op jit(solution)/shard_map/while/body/eval_jaxpr/ppermute | solution.py:9
  789.2 13.9 conditional.10
  960.7 19.2 %collective-permute-start = (bf16[16,4096]{1,0:T(8,128)(2,1)}, bf16[16,4096]{1,0:T(8,128)(2,1)S(1)}, u32[]{:S(2)}, u32[]{:S(2)}) collective-permute-start(bf16[16,4096]{1,0:T(8,128)(2,1)} %get-tuple-element.654), channel_id=1, source_target_pairs={{0,8},{8,16},{16,24},{24,32},{32,40},{40,48},{48,56},{56,64},{64,7... | collective-permute-start | bytes 393224 | tf_op jit(solution)/shard_map/while/body/eval_jaxpr/ppermute | solution.py:9
  1201.1 117.8 %collective-permute-done = bf16[16,4096]{1,0:T(8,128)(2,1)S(1)} collective-permute-done((bf16[16,4096]{1,0:T(8,128)(2,1)}, bf16[16,4096]{1,0:T(8,128)(2,1)S(1)}, u32[]{:S(2)}, u32[]{:S(2)}) %collective-permute-start) | collective-permute-done | bytes 131104 | tf_op jit(solution)/shard_map/while/body/eval_jaxpr/ppermute | solution.py:9
  1318.9 13.9 conditional.10
  1341.0 13.9 conditional.10
  1363.1 13.9 conditional.10
  1385.2 13.9 conditional.10
  1407.3 13.9 conditional.10
  1429.4 13.9 conditional.10
  1451.5 13.9 conditional.10
  1473.6 13.9 conditional.10
  (583 shorter events, 1172.8 us)
Async XLA Ops:
  6.5 87.8 %all-gather.3.cloned.1.call-start = ((), (), s32[]{:S(2)}) async-start(), calls=%async_computation | async-start | bytes 8257536 | tf_op jit(solution)/shard_map/all_gather | solution.py:83
  7.3 260.7 %all-gather.5.cloned.1.call-start = ((), (), s32[]{:S(2)}) async-start(), calls=%async_computation.1 | async-start | bytes 18874368 | tf_op jit(solution)/shard_map/all_gather | solution.py:85
  282.1 16.0 %collective-permute-start = (bf16[16,4096]{1,0:T(8,128)(2,1)}, bf16[16,4096]{1,0:T(8,128)(2,1)S(1)}, u32[]{:S(2)}, u32[]{:S(2)}) collective-permute-start(bf16[16,4096]{1,0:T(8,128)(2,1)} %get-tuple-element.654), channel_id=1, source_target_pairs={{0,8},{8,16},{16,24},{24,32},{32,40},{40,48},{48,56},{56,64},{64,7... | collective-permute-start | bytes 393224 | tf_op jit(solution)/shard_map/while/body/eval_jaxpr/ppermute | solution.py:9
  298.7 21.4 %collective-permute-start = (bf16[16,4096]{1,0:T(8,128)(2,1)}, bf16[16,4096]{1,0:T(8,128)(2,1)S(1)}, u32[]{:S(2)}, u32[]{:S(2)}) collective-permute-start(bf16[16,4096]{1,0:T(8,128)(2,1)} %get-tuple-element.654), channel_id=1, source_target_pairs={{0,8},{8,16},{16,24},{24,32},{32,40},{40,48},{48,56},{56,64},{64,7... | collective-permute-start | bytes 393224 | tf_op jit(solution)/shard_map/while/body/eval_jaxpr/ppermute | solution.py:9
  320.8 21.4 %collective-permute-start = (bf16[16,4096]{1,0:T(8,128)(2,1)}, bf16[16,4096]{1,0:T(8,128)(2,1)S(1)}, u32[]{:S(2)}, u32[]{:S(2)}) collective-permute-start(bf16[16,4096]{1,0:T(8,128)(2,1)} %get-tuple-element.654), channel_id=1, source_target_pairs={{0,8},{8,16},{16,24},{24,32},{32,40},{40,48},{48,56},{56,64},{64,7... | collective-permute-start | bytes 393224 | tf_op jit(solution)/shard_map/while/body/eval_jaxpr/ppermute | solution.py:9
  342.9 21.4 %collective-permute-start = (bf16[16,4096]{1,0:T(8,128)(2,1)}, bf16[16,4096]{1,0:T(8,128)(2,1)S(1)}, u32[]{:S(2)}, u32[]{:S(2)}) collective-permute-start(bf16[16,4096]{1,0:T(8,128)(2,1)} %get-tuple-element.654), channel_id=1, source_target_pairs={{0,8},{8,16},{16,24},{24,32},{32,40},{40,48},{48,56},{56,64},{64,7... | collective-permute-start | bytes 393224 | tf_op jit(solution)/shard_map/while/body/eval_jaxpr/ppermute | solution.py:9
  365.0 21.4 %collective-permute-start = (bf16[16,4096]{1,0:T(8,128)(2,1)}, bf16[16,4096]{1,0:T(8,128)(2,1)S(1)}, u32[]{:S(2)}, u32[]{:S(2)}) collective-permute-start(bf16[16,4096]{1,0:T(8,128)(2,1)} %get-tuple-element.654), channel_id=1, source_target_pairs={{0,8},{8,16},{16,24},{24,32},{32,40},{40,48},{48,56},{56,64},{64,7... | collective-permute-start | bytes 393224 | tf_op jit(solution)/shard_map/while/body/eval_jaxpr/ppermute | solution.py:9
  387.1 21.4 %collective-permute-start = (bf16[16,4096]{1,0:T(8,128)(2,1)}, bf16[16,4096]{1,0:T(8,128)(2,1)S(1)}, u32[]{:S(2)}, u32[]{:S(2)}) collective-permute-start(bf16[16,4096]{1,0:T(8,128)(2,1)} %get-tuple-element.654), channel_id=1, source_target_pairs={{0,8},{8,16},{16,24},{24,32},{32,40},{40,48},{48,56},{56,64},{64,7... | collective-permute-start | bytes 393224 | tf_op jit(solution)/shard_map/while/body/eval_jaxpr/ppermute | solution.py:9
  409.2 21.4 %collective-permute-start = (bf16[16,4096]{1,0:T(8,128)(2,1)}, bf16[16,4096]{1,0:T(8,128)(2,1)S(1)}, u32[]{:S(2)}, u32[]{:S(2)}) collective-permute-start(bf16[16,4096]{1,0:T(8,128)(2,1)} %get-tuple-element.654), channel_id=1, source_target_pairs={{0,8},{8,16},{16,24},{24,32},{32,40},{40,48},{48,56},{56,64},{64,7... | collective-permute-start | bytes 393224 | tf_op jit(solution)/shard_map/while/body/eval_jaxpr/ppermute | solution.py:9
  431.2 21.4 %collective-permute-start = (bf16[16,4096]{1,0:T(8,128)(2,1)}, bf16[16,4096]{1,0:T(8,128)(2,1)S(1)}, u32[]{:S(2)}, u32[]{:S(2)}) collective-permute-start(bf16[16,4096]{1,0:T(8,128)(2,1)} %get-tuple-element.654), channel_id=1, source_target_pairs={{0,8},{8,16},{16,24},{24,32},{32,40},{40,48},{48,56},{56,64},{64,7... | collective-permute-start | bytes 393224 | tf_op jit(solution)/shard_map/while/body/eval_jaxpr/ppermute | solution.py:9
  453.3 8.2 collective-permute-start
  479.9 11.4 collective-permute-start
  518.6 11.4 collective-permute-start
  557.3 11.4 collective-permute-start
  596.0 12.6 collective-permute-start
  635.8 11.4 collective-permute-start
  665.6 123.6 %collective-permute-start = (bf16[16,4096]{1,0:T(8,128)(2,1)}, bf16[16,4096]{1,0:T(8,128)(2,1)S(1)}, u32[]{:S(2)}, u32[]{:S(2)}) collective-permute-start(bf16[16,4096]{1,0:T(8,128)(2,1)} %get-tuple-element.654), channel_id=1, source_target_pairs={{0,8},{8,16},{16,24},{24,32},{32,40},{40,48},{48,56},{56,64},{64,7... | collective-permute-start | bytes 393224 | tf_op jit(solution)/shard_map/while/body/eval_jaxpr/ppermute | solution.py:9
  960.7 21.4 %collective-permute-start = (bf16[16,4096]{1,0:T(8,128)(2,1)}, bf16[16,4096]{1,0:T(8,128)(2,1)S(1)}, u32[]{:S(2)}, u32[]{:S(2)}) collective-permute-start(bf16[16,4096]{1,0:T(8,128)(2,1)} %get-tuple-element.654), channel_id=1, source_target_pairs={{0,8},{8,16},{16,24},{24,32},{32,40},{40,48},{48,56},{56,64},{64,7... | collective-permute-start | bytes 393224 | tf_op jit(solution)/shard_map/while/body/eval_jaxpr/ppermute | solution.py:9
  1009.4 11.4 collective-permute-start
  1048.1 11.4 collective-permute-start
  1086.8 11.4 collective-permute-start
  1125.4 12.6 collective-permute-start
  1165.3 11.4 collective-permute-start
  1195.2 123.7 %collective-permute-start = (bf16[16,4096]{1,0:T(8,128)(2,1)}, bf16[16,4096]{1,0:T(8,128)(2,1)S(1)}, u32[]{:S(2)}, u32[]{:S(2)}) collective-permute-start(bf16[16,4096]{1,0:T(8,128)(2,1)} %get-tuple-element.654), channel_id=1, source_target_pairs={{0,8},{8,16},{16,24},{24,32},{32,40},{40,48},{48,56},{56,64},{64,7... | collective-permute-start | bytes 393224 | tf_op jit(solution)/shard_map/while/body/eval_jaxpr/ppermute | solution.py:9
  (49 other events, 390.8 us)
Sparse Core Ops, SparseCore 0:
  9.1 85.1 all-gather.2
  96.1 171.8 all-gather.4
where the time goes:
time: 1510 us; the launch traced here: 1500 us
  waiting for transfers between devices  678 us (45%)
  starting transfers between devices  476 us (32%)
  matrix products  124 us (8%)
  local copies, waits for them, and re-layouts  111 us (7%)
  blocking collectives  47.4 us (3%)
  other arithmetic  45 us (3%)
    ppermute x71, starting transfers between devices, shifted(): lax.ppermute(array, axis, [(i, (i + by) % size) for i in range(size)])  476 us
    ppermute x71, waiting for transfers between devices, shifted(): lax.ppermute(array, axis, [(i, (i + by) % size) for i in range(size)])  475 us
    all_gather x1, waiting for transfers between devices, shards(): lax.all_gather(out_blocks, 'dp', axis=2, tiled=True)  164 us
    dot_general x16, matrix products, apply_layer(): jnp.einsum('rjkc,jkcd->rjd', second, back_weight, preferred_element_type=...  73.4 us
    dot_general x16, matrix products, apply_layer(): jnp.einsum('rjkc,jkcd->rjd', picked, proj_weight, preferred_element_type=...  50.8 us
    another operation x72, local copies, waits for them, and re-layouts  50 us
    all_gather x1, waiting for transfers between devices, shards(): lax.all_gather(in_blocks, 'dp', axis=2, tiled=True)  37 us
  transfers between devices with their start and end apart: 73, of which 73 were waited for; matrix products, arithmetic and copies ran while one was open for 1% of the time, Pallas kernels for 0%

commit v1 on v0

v1 whole, which is shorter than its diff:
```python
import functools

import jax
import jax.numpy as jnp
from jax import lax
from jax.experimental import pallas as pl
from jax.experimental.pallas import tpu as pltpu
from jax.sharding import PartitionSpec as P

MESH = pl.DeviceIdType.MESH
BLOCK = 128
IN_PER = 14
OUT_PER = 4
K_OUT = 8
PER = IN_PER + OUT_PER * K_OUT
DB = 32
FB = 112
MICRO = 8
ROWS = 16
STAGES = 32
A1, A2, B1, B2 = (0, 11), (11, 10), (21, 13), (34, 12)
A, B = (0, 21), (21, 25)


def layer(x_ref, y_ref, held_ref, hid_ref, w_ref, ids_ref):
    sums = [jnp.zeros((ROWS, BLOCK), jnp.float32) for _ in range(4)]
    for j in range(DB):
        held_ref[j] = x_ref[j]
        v = x_ref[j].astype(jnp.float32)
        sums[j % 4] = sums[j % 4] + v * v
    total = (sums[0] + sums[1]) + (sums[2] + sums[3])
    mean = jnp.sum(total, axis=-1, keepdims=True) * (1.0 / (DB * BLOCK))
    scale = jnp.broadcast_to(lax.rsqrt(mean + 1e-05), (ROWS, BLOCK))
    for j in range(0, FB, 2):
        rows, mats = [], []
        for q in (j, j + 1):
            g, b = q // IN_PER, q % IN_PER
            rows.append(held_ref[ids_ref[g, 0, b]])
            mats.append(w_ref[g, b])
        both = jnp.dot(
            jnp.concatenate(rows, axis=0),
            jnp.concatenate(mats, axis=1),
            preferred_element_type=jnp.float32,
        )
        for q in range(2):
            p = both[q * ROWS : (q + 1) * ROWS, q * BLOCK : (q + 1) * BLOCK] * scale
            hid_ref[j + q] = (p / (1.0 + jnp.exp(-p))).astype(jnp.bfloat16)
    for j in range(DB):
        g, b = j // OUT_PER, IN_PER + (j % OUT_PER) * K_OUT
        picked = jnp.concatenate([hid_ref[ids_ref[g, 0, b + k]] for k in range(K_OUT)], axis=1)
        mat = w_ref[g, pl.ds(b, K_OUT)].reshape(K_OUT * BLOCK, BLOCK)
        back = jnp.dot(picked, mat, preferred_element_type=jnp.float32)
        y_ref[j] = (x_ref[j].astype(jnp.float32) + back).astype(jnp.bfloat16)


def relay(
    x_hbm, in_hbm, out_hbm, ids_hbm, res_hbm,
    w, act, held, hid, ids_vmem, ids_smem,
    load_sem, swap_send, swap_recv, ids_send, ids_recv, ids_local,
    ring_send, ring_recv, hop_send, hop_recv, res_send, res_recv, res_local, go_sem,
):
    section = lax.axis_index("section")
    dp = lax.axis_index("dp")
    m, core = section // 2, section % 2
    other = 1 - core
    x, y = dp % 4, dp // 4
    xr, xl, x2 = (x + 1) % 4, (x + 3) % 4, (x + 2) % 4
    stage = m + 16 * core
    nxt = (stage + 1) % STAGES
    prv = (stage + STAGES - 1) % STAGES
    next_section = 2 * (nxt % 16) + nxt // 16
    prev_section = 2 * (prv % 16) + prv // 16
    twin = (2 * m + other, dp)

    barrier = pltpu.get_barrier_semaphore()
    for d in range(1, 8):
        for c in range(2):
            pl.semaphore_signal(barrier, inc=1, device_id=(2 * m + c, (dp + d) % 8), device_id_type=MESH)
    pl.semaphore_signal(barrier, inc=1, device_id=twin, device_id_type=MESH)
    pl.semaphore_signal(barrier, inc=1, device_id=(next_section, dp), device_id_type=MESH)
    pl.semaphore_signal(barrier, inc=1, device_id=(prev_section, dp), device_id_type=MESH)
    pl.semaphore_wait(barrier, 17)

    mine = [
        pltpu.make_async_copy(in_hbm.at[core], w.at[core, dp, pl.ds(0, IN_PER)], load_sem.at[0]),
        pltpu.make_async_copy(out_hbm.at[core], w.at[core, dp, pl.ds(IN_PER, PER - IN_PER)], load_sem.at[1]),
    ]
    swaps = [
        pltpu.make_async_remote_copy(
            in_hbm.at[other], w.at[core, dp, pl.ds(0, IN_PER)],
            swap_send.at[0], swap_recv.at[0], device_id=twin, device_id_type=MESH),
        pltpu.make_async_remote_copy(
            out_hbm.at[other], w.at[core, dp, pl.ds(IN_PER, PER - IN_PER)],
            swap_send.at[1], swap_recv.at[1], device_id=twin, device_id_type=MESH),
    ]
    for c in mine + swaps:
        c.start()
    landed = [
        pltpu.make_async_remote_copy(
            in_hbm.at[other], w.at[other, dp, pl.ds(0, IN_PER)],
            swap_send.at[0], swap_recv.at[0], device_id=twin, device_id_type=MESH),
        pltpu.make_async_remote_copy(
            out_hbm.at[other], w.at[other, dp, pl.ds(IN_PER, PER - IN_PER)],
            swap_send.at[1], swap_recv.at[1], device_id=twin, device_id_type=MESH),
    ]
    id_own = pltpu.make_async_copy(ids_hbm.at[core], ids_vmem.at[core, dp], ids_local.at[0])
    id_own.start()
    id_copies = []
    for d in range(8):
        peer = (dp + d) % 8
        if d:
            id_copies.append(pltpu.make_async_remote_copy(
                ids_hbm.at[core], ids_vmem.at[core, dp], ids_send.at[2 * d], ids_recv.at[2 * d],
                device_id=(section, peer), device_id_type=MESH))
        id_copies.append(pltpu.make_async_remote_copy(
            ids_hbm.at[other], ids_vmem.at[core, dp], ids_send.at[2 * d + 1], ids_recv.at[2 * d + 1],
            device_id=(2 * m + other, peer), device_id_type=MESH))
    for c in id_copies:
        c.start()
    load_x = pltpu.make_async_copy(x_hbm, act.at[0], load_sem.at[2])

    @pl.when(stage == 0)
    def _():
        load_x.start()

    for c in mine:
        c.wait()
    for c in landed:
        c.wait_recv()

    @pl.when(core == 1)
    def _():
        pl.semaphore_wait(go_sem, 1)

    def at(px, py):
        return py * 4 + px

    to = {
        "r": (section, at(xr, y)),
        "l": (section, at(xl, y)),
        "y": (section, at(x, 1 - y)),
    }
    here, across = at(x, y), at(x, 1 - y)
    plan = [
        ("r", here, A), ("r", here, B), ("r", at(xl, y), A1), ("r", across, B), ("r", at(xl, y), B1), ("r", at(xl, 1 - y), B1),
        ("l", here, A), ("l", here, B), ("l", at(xr, y), A2), ("l", across, B), ("l", at(xr, y), B2), ("l", at(xr, 1 - y), B2),
        ("y", here, B), ("y", here, A), ("y", at(xl, y), A), ("y", at(xr, y), A), ("y", at(x2, y), A1), ("y", at(x2, y), A2),
    ]
    arrive = [
        (at(xl, y), A), (at(xl, y), B), (at(x2, y), A1), (at(xl, 1 - y), B), (at(x2, y), B1), (at(x2, 1 - y), B1),
        (at(xr, y), A), (at(xr, y), B), (at(x2, y), A2), (at(xr, 1 - y), B), (at(x2, y), B2), (at(x2, 1 - y), B2),
        (across, B), (across, A), (at(xl, 1 - y), A), (at(xr, 1 - y), A), (at(x2, 1 - y), A1), (at(x2, 1 - y), A2),
    ]

    def piece(l, t, where):
        g, (first, count) = where
        part = w.at[l, g, pl.ds(first, count)]
        return pltpu.make_async_remote_copy(
            part, part, ring_send.at[l, t], ring_recv.at[l, t], device_id=to[plan[t][0]], device_id_type=MESH)

    def send(l, t):
        piece(l, t, plan[t][1:]).start()

    def got(l, t):
        piece(l, t, arrive[t]).wait_recv()

    for l in range(2):
        for t in (0, 6, 12, 1, 7, 13):
            send(l, t)
    first = [(0, (2, 14)), (6, (8, 15)), (12, (3, 9)), (1, (4,)), (7, (10,)), (13, ())]
    second = [(2, (16,)), (8, (17,)), (3, (5,)), (9, (11,))]
    last = [(t, ()) for t in (4, 10, 14, 15, 5, 11, 16, 17)]
    for group in (first, second, last):
        for l in range(2):
            for t, then in group:
                got(l, t)
                for s in then:
                    send(l, s)
    for l in range(2):
        for t in range(18):
            piece(l, t, plan[t][1:]).wait_send()

    @pl.when(core == 0)
    def _():
        pl.semaphore_signal(go_sem, inc=1, device_id=twin, device_id_type=MESH)

    for c in swaps:
        c.wait_send()
    id_own.wait()
    for d in range(8):
        back = (dp + 8 - d) % 8
        if d:
            pltpu.make_async_remote_copy(
                ids_hbm.at[core], ids_vmem.at[core, back], ids_send.at[2 * d], ids_recv.at[2 * d],
                device_id=(section, back), device_id_type=MESH).wait_recv()
        pltpu.make_async_remote_copy(
            ids_hbm.at[core], ids_vmem.at[other, back], ids_send.at[2 * d + 1], ids_recv.at[2 * d + 1],
            device_id=(2 * m + other, back), device_id_type=MESH).wait_recv()
    for c in id_copies:
        c.wait_send()
    fetch = pltpu.make_async_copy(ids_vmem, ids_smem, ids_local.at[0])
    fetch.start()
    fetch.wait()

    @pl.when(stage == 0)
    def _():
        load_x.wait()

    def hop(i):
        return pltpu.make_async_remote_copy(
            act.at[2, i], act.at[0, i], hop_send.at[i], hop_recv.at[i],
            device_id=(next_section, dp), device_id_type=MESH)

    def result_local(i):
        return pltpu.make_async_copy(act.at[1 + core, i], res_hbm.at[core, i], res_local.at[i])

    def result_remote(i):
        return pltpu.make_async_remote_copy(
            act.at[2 - core, i], res_hbm.at[core, i], res_send.at[i], res_recv.at[i],
            device_id=twin, device_id_type=MESH)

    def result_landed(i):
        return pltpu.make_async_remote_copy(
            act.at[2 - core, i], res_hbm.at[other, i], res_send.at[i], res_recv.at[i],
            device_id=twin, device_id_type=MESH)

    def step(t, carry):
        i, l = t // 2, t % 2

        @pl.when((l == 0) & (stage > 0))
        def _():
            hop(i).wait_recv()

        layer(act.at[l, i], act.at[l + 1, i], held, hid, w.at[l], ids_smem.at[l])

        @pl.when((l == 1) & (stage < STAGES - 1))
        def _():
            hop(i).start()

        @pl.when(l == core)
        def _():
            result_local(i).start()

        @pl.when(l != core)
        def _():
            result_remote(i).start()

        return carry

    lax.fori_loop(0, 2 * MICRO, step, 0)

    def finish(i, carry):
        @pl.when(stage < STAGES - 1)
        def _():
            hop(i).wait_send()

        result_local(i).wait()
        result_remote(i).wait_send()
        result_landed(i).wait_recv()
        return carry

    lax.fori_loop(0, MICRO, finish, 0)


def shards(inputs, in_blocks, in_ids, out_blocks, out_ids):
    x = inputs.reshape(MICRO, ROWS, DB, BLOCK).transpose(0, 2, 1, 3)
    w_in = in_blocks.reshape(2, IN_PER, BLOCK, BLOCK)
    w_out = out_blocks.reshape(2, OUT_PER * K_OUT, BLOCK, BLOCK)
    ids = jnp.concatenate(
        [
            in_ids.reshape(2, 1, IN_PER),
            out_ids.reshape(2, 1, OUT_PER * K_OUT),
            jnp.zeros((2, 1, BLOCK - PER), jnp.int32),
        ],
        axis=2,
    )
    dma = pltpu.SemaphoreType.DMA
    result = pl.pallas_call(
        relay,
        out_shape=jax.ShapeDtypeStruct((2, MICRO, DB, ROWS, BLOCK), jnp.bfloat16),
        in_specs=[pl.BlockSpec(memory_space=pl.ANY)] * 4,
        out_specs=pl.BlockSpec(memory_space=pl.ANY),
        scratch_shapes=[
            pltpu.VMEM((2, 8, PER, BLOCK, BLOCK), jnp.bfloat16),
            pltpu.VMEM((3, MICRO, DB, ROWS, BLOCK), jnp.bfloat16),
            pltpu.VMEM((DB, ROWS, BLOCK), jnp.bfloat16),
            pltpu.VMEM((FB, ROWS, BLOCK), jnp.bfloat16),
            pltpu.VMEM((2, 8, 1, BLOCK), jnp.int32),
            pltpu.SMEM((2, 8, 1, BLOCK), jnp.int32),
            dma((3,)), dma((2,)), dma((2,)), dma((16,)), dma((16,)), dma((1,)),
            dma((2, 18)), dma((2, 18)), dma((MICRO,)), dma((MICRO,)),
            dma((MICRO,)), dma((MICRO,)), dma((MICRO,)),
            pltpu.SemaphoreType.REGULAR,
        ],
        compiler_params=pltpu.CompilerParams(
            collective_id=0, has_side_effects=True, vmem_limit_bytes=60 * 2**20
        ),
    )(x, w_in, w_out, ids)
    result = result.transpose(0, 1, 3, 2, 4).reshape(2, 1, MICRO, ROWS, DB * BLOCK)
    return result


def solution(mesh):
    return jax.shard_map(
        shards,
        mesh=mesh,
        in_specs=(
            P(None, "dp", None),
            P(None, "section", "dp", None, None, None),
            P(None, "section", "dp", None),
            P(None, "section", "dp", None, None, None),
            P(None, "section", "dp", None),
        ),
        out_specs=P(None, "section", None, "dp", None),
        check_vma=False,
    )
```

time: 1510 us -> 363 us (0.24)
  waiting for transfers between devices: 678 us -> 0 us
  starting transfers between devices: 476 us -> 0 us
  Pallas kernels: 0 us -> 355 us
  matrix products: 124 us -> 0 us
  local copies, waits for them, and re-layouts: 111 us -> 6.5 us
  blocking collectives: 47.4 us -> 0 us
  other arithmetic: 45 us -> 1.33 us
    ppermute x71 -> x0, starting transfers between devices: 476 us -> none  [shifted(): lax.ppermute(array, axis, [(i, (i + by) % size) for i in range(size)])]
    ppermute x71 -> x0, waiting for transfers between devices: 475 us -> none  [shifted(): lax.ppermute(array, axis, [(i, (i + by) % size) for i in range(size)])]
    pallas_call x0 -> x1, Pallas kernels: none -> 355 us  [shards(): pl.pallas_call(relay, out_shape=jax.ShapeDtypeStruct((2, MICRO, DB, ROWS,...]
    all_gather x2 -> x0, waiting for transfers between devices: 201 us -> none  [the longest x1 164 us: shards(): lax.all_gather(out_blocks, 'dp', axis=2, tiled=True)]
    dot_general x32 -> x0, matrix products: 124 us -> none  [the longest x16 73.4 us: apply_layer(): jnp.einsum('rjkc,jkcd->rjd', second, back_weight, preferred_element_type=...]
    another operation x88 -> x0, local copies, waits for them, and re-layouts: 51.4 us -> none
    all_gather x2 -> x0, blocking collectives: 47.4 us -> none  [the longest x1 24.3 us: shards(): lax.all_gather(out_ids, 'dp', axis=2, tiled=True)]
    select_n x64 -> x0, other arithmetic: 29.7 us -> none  [the longest x48 14.9 us: select_blocks(): picked = jnp.take(blocks, block_ids.reshape(-1), axis=1)]
  transfers between devices with their start and end apart: 73 -> 0, of which waited for: 73 -> 0; matrix products, arithmetic and copies ran while one was open for 1% -> 0% of each run, Pallas kernels for 0% -> 0%
where the time goes in v1:
time: 363 us
  Pallas kernels  355 us (98%)
  local copies, waits for them, and re-layouts  6.5 us (2%)
    pallas_call x1, Pallas kernels, shards(): pl.pallas_call(relay, out_shape=jax.ShapeDtypeStruct((2, MICRO, DB, ROWS,...  355 us

profile of v1, /device:TPU:241, one launch (start us, length us, event | category | flops | bytes accessed | tf_op | source)
XLA Modules:
  0.0 363.1 jit_solution(1447056728812654866)
XLA Ops:
  0.0 0.0 copy-start
  0.0 0.1 pad.2.clone
  0.1 0.8 reshape.22
  0.9 1.3 add_add_fusion.ids_hbm
  2.3 0.0 copy-done
  2.3 1.2 bitcast_bitcast_fusion.x_hbm
  3.4 355.2 %shard_map.55 = bf16[2,8,32,16,128]{4,3,2,1,0:T(8,128)(2,1)} custom-call(bf16[8,32,16,128]{3,2,1,0:T(8,128)(2,1)} %bitcast_bitcast_fusion.x_hbm, bf16[2,14,128,128]{3,2,1,0:T(8,128)(2,1)} %bitcast.19, bf16[2,32,128,128]{3,2,1,0:T(8,128)(2,1)} %bitcast.18, s32[2,1,128]{2,1,0:T(1,128)} %add_add_fusion.ids_hbm), custom_call_target="tpu_custom_call" | custom-call | tf_op jit(solution)/shard_map/pallas_call | solution.py:278
  358.6 2.1 copy.11
  360.8 2.3 reshape.23
  (1 shorter events, 0.0 us)
Async XLA Ops:
  0.0 2.3 copy-start

commit v2 on v1

v2 whole, which is shorter than its diff:
```python
import functools

import jax
import jax.numpy as jnp
from jax import lax
from jax.experimental import pallas as pl
from jax.experimental.pallas import tpu as pltpu
from jax.sharding import PartitionSpec as P

MESH = pl.DeviceIdType.MESH
BLOCK = 128
IN_PER = 14
OUT_PER = 4
K_OUT = 8
PER = IN_PER + OUT_PER * K_OUT
DB = 32
FB = 112
MICRO = 8
ROWS = 16
STAGES = 32
LAG = 4
PIECE = 4
A1, A2, B1, B2 = (0, 11), (11, 10), (21, 13), (34, 12)
A, B = (0, 21), (21, 25)


def layer(x_ref, y_ref, held_ref, hid_ref, w_ref, ids_ref, emit):
    sums = [jnp.zeros((ROWS, BLOCK), jnp.float32) for _ in range(4)]
    for j in range(DB):
        held_ref[j] = x_ref[j]
        v = x_ref[j].astype(jnp.float32)
        sums[j % 4] = sums[j % 4] + v * v
    total = (sums[0] + sums[1]) + (sums[2] + sums[3])
    mean = jnp.sum(total, axis=-1, keepdims=True) * (1.0 / (DB * BLOCK))
    scale = jnp.broadcast_to(lax.rsqrt(mean + 1e-05), (ROWS, BLOCK))
    for j in range(0, FB, 2):
        rows, mats = [], []
        for q in (j, j + 1):
            g, b = q // IN_PER, q % IN_PER
            rows.append(held_ref[ids_ref[g, 0, b]])
            mats.append(w_ref[g, b])
        both = jnp.dot(
            jnp.concatenate(rows, axis=0),
            jnp.concatenate(mats, axis=1),
            preferred_element_type=jnp.float32,
        )
        for q in range(2):
            p = both[q * ROWS : (q + 1) * ROWS, q * BLOCK : (q + 1) * BLOCK] * scale
            hid_ref[j + q] = (p / (1.0 + jnp.exp(-p))).astype(jnp.bfloat16)
    backs = {}
    for step in range(DB + LAG):
        if step < DB:
            g, b = step // OUT_PER, IN_PER + (step % OUT_PER) * K_OUT
            picked = jnp.concatenate([hid_ref[ids_ref[g, 0, b + k]] for k in range(K_OUT)], axis=1)
            mat = w_ref[g, pl.ds(b, K_OUT)].reshape(K_OUT * BLOCK, BLOCK)
            backs[step] = jnp.dot(picked, mat, preferred_element_type=jnp.float32)
        j = step - LAG
        if j >= 0:
            y_ref[j] = (x_ref[j].astype(jnp.float32) + backs.pop(j)).astype(jnp.bfloat16)
            if emit is not None and (j + 1) % PIECE == 0:
                emit(j + 1 - PIECE)


def relay(
    x_hbm, in_hbm, out_hbm, ids_hbm, res_hbm,
    w, act, held, hid, ids_vmem, ids_smem,
    load_sem, swap_send, swap_recv, ids_send, ids_recv, ids_local,
    ring_send, ring_recv, hop_send, hop_recv, res_send, res_recv, res_local, go_sem,
):
    section = lax.axis_index("section")
    dp = lax.axis_index("dp")
    m, core = section // 2, section % 2
    other = 1 - core
    x, y = dp % 4, dp // 4
    xr, xl, x2 = (x + 1) % 4, (x + 3) % 4, (x + 2) % 4
    stage = m + 16 * core
    nxt = (stage + 1) % STAGES
    prv = (stage + STAGES - 1) % STAGES
    next_section = 2 * (nxt % 16) + nxt // 16
    prev_section = 2 * (prv % 16) + prv // 16
    twin = (2 * m + other, dp)

    barrier = pltpu.get_barrier_semaphore()
    for d in range(1, 8):
        for c in range(2):
            pl.semaphore_signal(barrier, inc=1, device_id=(2 * m + c, (dp + d) % 8), device_id_type=MESH)
    pl.semaphore_signal(barrier, inc=1, device_id=twin, device_id_type=MESH)
    pl.semaphore_signal(barrier, inc=1, device_id=(next_section, dp), device_id_type=MESH)
    pl.semaphore_signal(barrier, inc=1, device_id=(prev_section, dp), device_id_type=MESH)
    pl.semaphore_wait(barrier, 17)

    def at(px, py):
        return py * 4 + px

    here, across = at(x, y), at(x, 1 - y)
    plan = [
        ("r", here, A), ("r", here, B), ("r", at(xl, y), A1), ("r", across, B), ("r", at(xl, y), B1), ("r", at(xl, 1 - y), B1),
        ("l", here, A), ("l", here, B), ("l", at(xr, y), A2), ("l", across, B), ("l", at(xr, y), B2), ("l", at(xr, 1 - y), B2),
        ("y", here, B), ("y", here, A), ("y", at(xl, y), A), ("y", at(xr, y), A), ("y", at(x2, y), A1), ("y", at(x2, y), A2),
    ]
    arrive = [
        (at(xl, y), A), (at(xl, y), B), (at(x2, y), A1), (at(xl, 1 - y), B), (at(x2, y), B1), (at(x2, 1 - y), B1),
        (at(xr, y), A), (at(xr, y), B), (at(x2, y), A2), (at(xr, 1 - y), B), (at(x2, y), B2), (at(x2, 1 - y), B2),
        (across, B), (across, A), (at(xl, 1 - y), A), (at(xr, 1 - y), A), (at(x2, 1 - y), A1), (at(x2, 1 - y), A2),
    ]

    def shard_to(lap, sems):
        return [
            (in_hbm.at[lap], w.at[core, dp, pl.ds(0, IN_PER)]) + tuple(sem.at[0] for sem in sems),
            (out_hbm.at[lap], w.at[core, dp, pl.ds(IN_PER, PER - IN_PER)]) + tuple(sem.at[1] for sem in sems),
        ]

    mine = [pltpu.make_async_copy(*spec) for spec in shard_to(core, (load_sem,))]
    swaps = [
        pltpu.make_async_remote_copy(*spec, device_id=twin, device_id_type=MESH)
        for spec in shard_to(other, (swap_send, swap_recv))
    ]
    landed = [
        pltpu.make_async_remote_copy(
            in_hbm.at[other], w.at[other, dp, pl.ds(0, IN_PER)],
            swap_send.at[0], swap_recv.at[0], device_id=twin, device_id_type=MESH),
        pltpu.make_async_remote_copy(
            out_hbm.at[other], w.at[other, dp, pl.ds(IN_PER, PER - IN_PER)],
            swap_send.at[1], swap_recv.at[1], device_id=twin, device_id_type=MESH),
    ]

    def toward(way, lap):
        px, py = {"r": (xr, y), "l": (xl, y), "y": (x, 1 - y)}[way]
        return (2 * m + lap, at(px, py))

    def send_own(lap):
        slot = jnp.where(lap == core, core, other)
        for t in (0, 6, 12, 1, 7, 13):
            parts = [(out_hbm.at[lap, pl.ds(7, 25)], pl.ds(B[0], B[1]))]
            if plan[t][2] == A:
                parts = [(in_hbm.at[lap], pl.ds(0, IN_PER)), (out_hbm.at[lap, pl.ds(0, 7)], pl.ds(IN_PER, 7))]
            for source, where in parts:
                pltpu.make_async_remote_copy(
                    source, w.at[core, dp, where], ring_send.at[slot, t], ring_recv.at[core, t],
                    device_id=toward(plan[t][0], lap), device_id_type=MESH).start()

    send_own(0)
    for c in mine + swaps:
        c.start()
    id_own = pltpu.make_async_copy(ids_hbm.at[core], ids_vmem.at[core, dp], ids_local.at[0])
    id_own.start()
    id_copies = []
    for d in range(8):
        peer = (dp + d) % 8
        if d:
            id_copies.append(pltpu.make_async_remote_copy(
                ids_hbm.at[core], ids_vmem.at[core, dp], ids_send.at[2 * d], ids_recv.at[2 * d],
                device_id=(section, peer), device_id_type=MESH))
        id_copies.append(pltpu.make_async_remote_copy(
            ids_hbm.at[other], ids_vmem.at[core, dp], ids_send.at[2 * d + 1], ids_recv.at[2 * d + 1],
            device_id=(2 * m + other, peer), device_id_type=MESH))
    for c in id_copies:
        c.start()
    load_x = [
        pltpu.make_async_copy(x_hbm.at[:, h], act.at[0, :, :, pl.ds(8 * h, 8)], load_sem.at[2 + h]) for h in range(2)
    ]

    @pl.when(stage == 0)
    def _():
        for c in load_x:
            c.start()

    @pl.when(core == 1)
    def _():
        pl.semaphore_wait(go_sem, 1)
        send_own(1)

    def piece(l, t, where):
        g, (first, count) = where
        part = w.at[l, g, pl.ds(first, count)]
        return pltpu.make_async_remote_copy(
            part, part, ring_send.at[l, t], ring_recv.at[l, t], device_id=toward(plan[t][0], core), device_id_type=MESH)

    def send(l, t):
        piece(l, t, plan[t][1:]).start()

    def got(l, t):
        piece(l, t, arrive[t]).wait_recv()

    first = [(0, (2, 14)), (6, (8, 15)), (12, (3, 9)), (1, (4,)), (7, (10,)), (13, ())]
    second = [(2, (16,)), (8, (17,)), (3, (5,)), (9, (11,))]
    last = [(t, ()) for t in (4, 10, 14, 15, 5, 11, 16, 17)]
    for group in (first, second, last):
        for l in range(2):
            for t, then in group:
                got(l, t)
                for s in then:
                    send(l, s)

    @pl.when(core == 0)
    def _():
        pl.semaphore_signal(go_sem, inc=1, device_id=twin, device_id_type=MESH)
        send_own(1)

    for c in mine:
        c.wait()
    for c in landed:
        c.wait_recv()
    id_own.wait()
    for d in range(8):
        back = (dp + 8 - d) % 8
        if d:
            pltpu.make_async_remote_copy(
                ids_hbm.at[core], ids_vmem.at[core, back], ids_send.at[2 * d], ids_recv.at[2 * d],
                device_id=(section, back), device_id_type=MESH).wait_recv()
        pltpu.make_async_remote_copy(
            ids_hbm.at[core], ids_vmem.at[other, back], ids_send.at[2 * d + 1], ids_recv.at[2 * d + 1],
            device_id=(2 * m + other, back), device_id_type=MESH).wait_recv()
    for c in id_copies:
        c.wait_send()
    fetch = pltpu.make_async_copy(ids_vmem, ids_smem, ids_local.at[0])
    fetch.start()
    fetch.wait()

    @pl.when(stage == 0)
    def _():
        for c in load_x:
            c.wait()

    def hop(i, spare):
        return pltpu.make_async_remote_copy(
            act.at[2, i], act.at[3 * spare, i], hop_send.at[i], hop_recv.at[spare, i],
            device_id=(next_section, dp), device_id_type=MESH)

    ends = jnp.where(stage == STAGES - 1, 1, 0)
    hop_to = (jnp.where(stage == STAGES - 1, 2 * m + other, next_section), dp)

    def send_hop(i, first):
        part = pl.ds(first, PIECE)
        pltpu.make_async_remote_copy(
            act.at[2, i, part], act.at[3 * ends, i, part], hop_send.at[i], hop_recv.at[ends, i],
            device_id=hop_to, device_id_type=MESH).start()

    def half(l, i, h):
        return act.at[l + 1, i, :, pl.ds(8 * h, 8)]

    def result_local(i, h):
        return pltpu.make_async_copy(half(core, i, h), res_hbm.at[core, i, h], res_local.at[i, h])

    def result_remote(i, h):
        return pltpu.make_async_remote_copy(
            half(other, i, h), res_hbm.at[core, i, h], res_send.at[i, h], res_recv.at[i, h],
            device_id=twin, device_id_type=MESH)

    def result_landed(i, h):
        return pltpu.make_async_remote_copy(
            half(other, i, h), res_hbm.at[other, i, h], res_send.at[i, h], res_recv.at[i, h],
            device_id=twin, device_id_type=MESH)

    def step(i, carry):
        @pl.when(stage > 0)
        def _():
            hop(i, 0).wait_recv()

        layer(act.at[0, i], act.at[1, i], held, hid, w.at[0], ids_smem.at[0], None)
        layer(act.at[1, i], act.at[2, i], held, hid, w.at[1], ids_smem.at[1], functools.partial(send_hop, i))
        for h in range(2):
            result_local(i, h).start()
            result_remote(i, h).start()
        return carry

    lax.fori_loop(0, MICRO, step, 0)

    def finish(i, carry):
        hop(i, 0).wait_send()

        @pl.when(stage == STAGES // 2 - 1)
        def _():
            hop(i, 1).wait_recv()

        for h in range(2):
            result_local(i, h).wait()
            result_remote(i, h).wait_send()
            result_landed(i, h).wait_recv()
        return carry

    for c in swaps:
        c.wait_send()
    for l in range(2):
        for t in range(18):
            piece(l, t, plan[t][1:]).wait_send()
    lax.fori_loop(0, MICRO, finish, 0)


def shards(inputs, in_blocks, in_ids, out_blocks, out_ids):
    x = inputs.reshape(MICRO, 2, 8, DB, BLOCK).transpose(0, 1, 3, 2, 4)
    w_in = in_blocks.reshape(2, IN_PER, BLOCK, BLOCK)
    w_out = out_blocks.reshape(2, OUT_PER * K_OUT, BLOCK, BLOCK)
    ids = jnp.concatenate(
        [
            in_ids.reshape(2, 1, IN_PER),
            out_ids.reshape(2, 1, OUT_PER * K_OUT),
            jnp.zeros((2, 1, BLOCK - PER), jnp.int32),
        ],
        axis=2,
    )
    dma = pltpu.SemaphoreType.DMA
    result = pl.pallas_call(
        relay,
        out_shape=jax.ShapeDtypeStruct((2, MICRO, 2, DB, 8, BLOCK), jnp.bfloat16),
        in_specs=[pl.BlockSpec(memory_space=pl.ANY)] * 4,
        out_specs=pl.BlockSpec(memory_space=pl.ANY),
        scratch_shapes=[
            pltpu.VMEM((2, 8, PER, BLOCK, BLOCK), jnp.bfloat16),
            pltpu.VMEM((4, MICRO, DB, ROWS, BLOCK), jnp.bfloat16),
            pltpu.VMEM((DB, ROWS, BLOCK), jnp.bfloat16),
            pltpu.VMEM((FB, ROWS, BLOCK), jnp.bfloat16),
            pltpu.VMEM((2, 8, 1, BLOCK), jnp.int32),
            pltpu.SMEM((2, 8, 1, BLOCK), jnp.int32),
            dma((4,)), dma((2,)), dma((2,)), dma((16,)), dma((16,)), dma((1,)),
            dma((2, 18)), dma((2, 18)), dma((MICRO,)), dma((2, MICRO)),
            dma((MICRO, 2)), dma((MICRO, 2)), dma((MICRO, 2)),
            pltpu.SemaphoreType.REGULAR,
        ],
        compiler_params=pltpu.CompilerParams(
            collective_id=0, has_side_effects=True, vmem_limit_bytes=60 * 2**20
        ),
    )(x, w_in, w_out, ids)
    result = result.transpose(0, 1, 2, 4, 3, 5).reshape(2, 1, MICRO, ROWS, DB * BLOCK)
    return result


def solution(mesh):
    return jax.shard_map(
        shards,
        mesh=mesh,
        in_specs=(
            P(None, "dp", None),
            P(None, "section", "dp", None, None, None),
            P(None, "section", "dp", None),
            P(None, "section", "dp", None, None, None),
            P(None, "section", "dp", None),
        ),
        out_specs=P(None, "section", None, "dp", None),
        check_vma=False,
    )
```

time: 363 us -> 330 us (0.909)
  Pallas kernels: 355 us -> 324 us
    pallas_call x1, Pallas kernels: 355 us -> 324 us  [shards(): pl.pallas_call(relay, out_shape=jax.ShapeDtypeStruct((2, MICRO, 2, DB, 8,...]
where the time goes in v2:
time: 330 us; the launch traced here: 329 us
  Pallas kernels  324 us (98%)
  local copies, waits for them, and re-layouts  3.98 us (1%)
    pallas_call x1, Pallas kernels, shards(): pl.pallas_call(relay, out_shape=jax.ShapeDtypeStruct((2, MICRO, 2, DB, 8,...  324 us

profile of v2, /device:TPU:241, one launch (start us, length us, event | category | flops | bytes accessed | tf_op | source)
XLA Modules:
  0.0 329.4 jit_solution(81092255054200753)
XLA Ops:
  0.0 0.1 pad.2.clone
  0.1 0.8 reshape.22
  0.8 1.3 add_add_fusion.ids_hbm
  2.2 324.1 %shard_map.55 = bf16[2,8,2,32,8,128]{5,4,3,2,1,0:T(8,128)(2,1)} custom-call(bf16[8,2,32,8,128]{4,3,2,1,0:T(8,128)(2,1)} %bitcast.14, bf16[2,14,128,128]{3,2,1,0:T(8,128)(2,1)} %bitcast.15, bf16[2,32,128,128]{3,2,1,0:T(8,128)(2,1)} %bitcast.13, s32[2,1,128]{2,1,0:T(1,128)} %add_add_fusion.ids_hbm), custom_call_target="tpu_custom_call" | custom-call | tf_op jit(solution)/shard_map/pallas_call | solution.py:303
  326.3 3.1 copy.9
  (1 shorter events, 0.0 us)

commit v3 on v2

--- a/solution.py
+++ b/solution.py
@@ -20,8 +20,14 @@
 STAGES = 32
 LAG = 4
 PIECE = 4
-A1, A2, B1, B2 = (0, 11), (11, 10), (21, 13), (34, 12)
-A, B = (0, 21), (21, 25)
+MAIN = {"A": (0, 17), "A1": (0, 9), "A2": (9, 8), "B": (17, 21), "B1": (17, 11), "B2": (28, 10)}
+REST = {"A": (38, 3), "A1": (38, 2), "A2": (40, 1), "B": (41, 5), "B1": (41, 3), "B2": (44, 2)}
+REST_AT, REST_LEN = 38, 8
+OWN = (0, 6, 12, 1, 7, 13)
+FIRST = ((0, (2, 14)), (6, (8, 15)), (12, (3, 9)), (1, (4,)), (7, (10,)), (13, ()))
+SECOND = ((2, (16,)), (8, (17,)), (3, (5,)), (9, (11,)))
+LAST = tuple((t, ()) for t in (4, 10, 14, 15, 5, 11, 16, 17))
+WAYS = "rrrrrrllllllyyyyyy"
 
 
 def layer(x_ref, y_ref, held_ref, hid_ref, w_ref, ids_ref, emit):
@@ -63,9 +69,10 @@
 
 def relay(
     x_hbm, in_hbm, out_hbm, ids_hbm, res_hbm,
-    w, act, held, hid, ids_vmem, ids_smem,
+    w, extra, act, held, hid, ids_vmem, ids_smem,
     load_sem, swap_send, swap_recv, ids_send, ids_recv, ids_local,
-    ring_send, ring_recv, hop_send, hop_recv, res_send, res_recv, res_local, go_sem,
+    ring_send, ring_recv, rest_send, rest_recv, extra_send, extra_recv, feed_send, feed_recv, back_send, back_recv,
+    hop_send, hop_recv, res_send, res_recv, res_local, go_sem,
 ):
     section = lax.axis_index("section")
     dp = lax.axis_index("dp")
@@ -79,6 +86,10 @@
     next_section = 2 * (nxt % 16) + nxt // 16
     prev_section = 2 * (prv % 16) + prv // 16
     twin = (2 * m + other, dp)
+    early = m < 8
+    partner = (2 * ((m + 8) % 16) + core, (dp + 4) % 8)
+    helped = (core == 0) & early
+    helps = (core == 0) & (m >= 8)
 
     barrier = pltpu.get_barrier_semaphore()
     for d in range(1, 8):
@@ -87,22 +98,28 @@
     pl.semaphore_signal(barrier, inc=1, device_id=twin, device_id_type=MESH)
     pl.semaphore_signal(barrier, inc=1, device_id=(next_section, dp), device_id_type=MESH)
     pl.semaphore_signal(barrier, inc=1, device_id=(prev_section, dp), device_id_type=MESH)
-    pl.semaphore_wait(barrier, 17)
+    for c in range(2):
+        pl.semaphore_signal(barrier, inc=1, device_id=(2 * ((m + 8) % 16) + c, (dp + 4) % 8), device_id_type=MESH)
+    pl.semaphore_wait(barrier, 19)
 
     def at(px, py):
         return py * 4 + px
 
-    here, across = at(x, y), at(x, 1 - y)
-    plan = [
-        ("r", here, A), ("r", here, B), ("r", at(xl, y), A1), ("r", across, B), ("r", at(xl, y), B1), ("r", at(xl, 1 - y), B1),
-        ("l", here, A), ("l", here, B), ("l", at(xr, y), A2), ("l", across, B), ("l", at(xr, y), B2), ("l", at(xr, 1 - y), B2),
-        ("y", here, B), ("y", here, A), ("y", at(xl, y), A), ("y", at(xr, y), A), ("y", at(x2, y), A1), ("y", at(x2, y), A2),
-    ]
-    arrive = [
-        (at(xl, y), A), (at(xl, y), B), (at(x2, y), A1), (at(xl, 1 - y), B), (at(x2, y), B1), (at(x2, 1 - y), B1),
-        (at(xr, y), A), (at(xr, y), B), (at(x2, y), A2), (at(xr, 1 - y), B), (at(x2, y), B2), (at(x2, 1 - y), B2),
-        (across, B), (across, A), (at(xl, 1 - y), A), (at(xr, 1 - y), A), (at(x2, 1 - y), A1), (at(x2, 1 - y), A2),
-    ]
+    def plan_of(parts, row):
+        def span(px, flip, name):
+            return at(px, 1 - row if flip else row), parts[name]
+
+        sends = [
+            span(x, 0, "A"), span(x, 0, "B"), span(xl, 0, "A1"), span(x, 1, "B"), span(xl, 0, "B1"), span(xl, 1, "B1"),
+            span(x, 0, "A"), span(x, 0, "B"), span(xr, 0, "A2"), span(x, 1, "B"), span(xr, 0, "B2"), span(xr, 1, "B2"),
+            span(x, 0, "B"), span(x, 0, "A"), span(xl, 0, "A"), span(xr, 0, "A"), span(x2, 0, "A1"), span(x2, 0, "A2"),
+        ]
+        arrivals = [
+            span(xl, 0, "A"), span(xl, 0, "B"), span(x2, 0, "A1"), span(xl, 1, "B"), span(x2, 0, "B1"), span(x2, 1, "B1"),
+            span(xr, 0, "A"), span(xr, 0, "B"), span(x2, 0, "A2"), span(xr, 1, "B"), span(x2, 0, "B2"), span(x2, 1, "B2"),
+            span(x, 1, "B"), span(x, 1, "A"), span(xl, 1, "A"), span(xr, 1, "A"), span(x2, 1, "A1"), span(x2, 1, "A2"),
+        ]
+        return sends, arrivals
 
     def shard_to(lap, sems):
         return [
@@ -128,18 +145,52 @@
         px, py = {"r": (xr, y), "l": (xl, y), "y": (x, 1 - y)}[way]
         return (2 * m + lap, at(px, py))
 
+    def own_copy(lap, way, first, count, send_sem, recv_sem):
+        if first == 0:
+            sources = [(in_hbm.at[lap], 0, IN_PER), (out_hbm.at[lap, pl.ds(0, count - IN_PER)], IN_PER, count - IN_PER)]
+        else:
+            sources = [(out_hbm.at[lap, pl.ds(first - IN_PER, count)], first, count)]
+        for source, start, length in sources:
+            pltpu.make_async_remote_copy(
+                source, w.at[core, dp, pl.ds(start, length)], send_sem, recv_sem,
+                device_id=toward(way, lap), device_id_type=MESH).start()
+
+    def feed(l):
+        return pltpu.make_async_remote_copy(
+            out_hbm.at[0, pl.ds(REST_AT - IN_PER, REST_LEN)], extra.at[l, dp], feed_send.at[0], feed_recv.at[l],
+            device_id=(2 * ((m + 8) % 16), (dp + 4) % 8), device_id_type=MESH)
+
     def send_own(lap):
         slot = jnp.where(lap == core, core, other)
-        for t in (0, 6, 12, 1, 7, 13):
-            parts = [(out_hbm.at[lap, pl.ds(7, 25)], pl.ds(B[0], B[1]))]
-            if plan[t][2] == A:
-                parts = [(in_hbm.at[lap], pl.ds(0, IN_PER)), (out_hbm.at[lap, pl.ds(0, 7)], pl.ds(IN_PER, 7))]
-            for source, where in parts:
-                pltpu.make_async_remote_copy(
-                    source, w.at[core, dp, where], ring_send.at[slot, t], ring_recv.at[core, t],
-                    device_id=toward(plan[t][0], lap), device_id_type=MESH).start()
-
-    send_own(0)
+
+        def main():
+            for t in OWN:
+                first, count = MAIN["A" if t in (0, 6, 13) else "B"]
+                own_copy(lap, WAYS[t], first, count, ring_send.at[slot, t], ring_recv.at[core, t])
+
+        def rest():
+            for t in OWN:
+                first, count = REST["A" if t in (0, 6, 13) else "B"]
+                own_copy(lap, WAYS[t], first, count, rest_send.at[slot, t], rest_recv.at[core, t])
+
+        if lap == 1:
+            main()
+            rest()
+        else:
+            @pl.when(early)
+            def _():
+                feed(core).start()
+
+            main()
+
+            @pl.when(m >= 8)
+            def _():
+                rest()
+
+    @pl.when(early)
+    def _():
+        send_own(0)
+
     for c in mine + swaps:
         c.start()
     id_own = pltpu.make_async_copy(ids_hbm.at[core], ids_vmem.at[core, dp], ids_local.at[0])
@@ -165,37 +216,95 @@
         for c in load_x:
             c.start()
 
+    def relay_over(buf, at_block, parts, row, send_sem, recv_sem):
+        sends, arrivals = plan_of(parts, row)
+
+        def piece(l, t, where):
+            g, (first, count) = where
+            part = buf.at[l, g, pl.ds(first - at_block, count)]
+            return pltpu.make_async_remote_copy(
+                part, part, send_sem.at[l, t], recv_sem.at[l, t],
+                device_id=toward(WAYS[t], core), device_id_type=MESH)
+
+        def start(l, t):
+            piece(l, t, sends[t]).start()
+
+        def run(groups, then=None):
+            for group in groups:
+                for l in range(2):
+                    for t, allows in group:
+                        piece(l, t, arrivals[t]).wait_recv()
+                        for k in allows:
+                            start(l, k)
+                        if then is not None:
+                            then(l, t)
+
+        def sent(l, t):
+            piece(l, t, sends[t]).wait_send()
+
+        return start, run, sent, arrivals
+
+    main_start, main_run, main_sent, _ = relay_over(w, 0, MAIN, y, ring_send, ring_recv)
+    rest_start, rest_run, rest_sent, rest_arrivals = relay_over(w, 0, REST, y, rest_send, rest_recv)
+    extra_start, extra_run, extra_sent, extra_arrivals = relay_over(extra, REST_AT, REST, 1 - y, extra_send, extra_recv)
+
+    def give_back(l, t):
+        g, (first, count) = extra_arrivals[t]
+        return pltpu.make_async_remote_copy(
+            extra.at[l, g, pl.ds(first - REST_AT, count)], w.at[l, g, pl.ds(first, count)],
+            back_send.at[l, t], back_recv.at[l, t], device_id=partner, device_id_type=MESH)
+
+    def given_back(l, t):
+        g, (first, count) = rest_arrivals[t]
+        return pltpu.make_async_remote_copy(
+            w.at[l, g, pl.ds(first, count)], w.at[l, g, pl.ds(first, count)],
+            back_send.at[l, t], back_recv.at[l, t], device_id=partner, device_id_type=MESH)
+
+    def fed(l):
+        client = (dp + 4) % 8
+        return pltpu.make_async_remote_copy(
+            extra.at[l, client], extra.at[l, client], feed_send.at[0], feed_recv.at[l],
+            device_id=partner, device_id_type=MESH)
+
+    def signal_twin():
+        pl.semaphore_signal(go_sem, inc=1, device_id=twin, device_id_type=MESH)
+
+    @pl.when(helps)
+    def _():
+        for l in range(2):
+            fed(l).wait_recv()
+            for t in OWN:
+                extra_start(l, t)
+        extra_run((FIRST, SECOND, LAST), lambda l, t: give_back(l, t).start())
+        signal_twin()
+        send_own(0)
+
+    @pl.when((core == 1) & (m >= 8))
+    def _():
+        pl.semaphore_wait(go_sem, 1)
+        send_own(0)
+
     @pl.when(core == 1)
     def _():
         pl.semaphore_wait(go_sem, 1)
         send_own(1)
 
-    def piece(l, t, where):
-        g, (first, count) = where
-        part = w.at[l, g, pl.ds(first, count)]
-        return pltpu.make_async_remote_copy(
-            part, part, ring_send.at[l, t], ring_recv.at[l, t], device_id=toward(plan[t][0], core), device_id_type=MESH)
-
-    def send(l, t):
-        piece(l, t, plan[t][1:]).start()
-
-    def got(l, t):
-        piece(l, t, arrive[t]).wait_recv()
-
-    first = [(0, (2, 14)), (6, (8, 15)), (12, (3, 9)), (1, (4,)), (7, (10,)), (13, ())]
-    second = [(2, (16,)), (8, (17,)), (3, (5,)), (9, (11,))]
-    last = [(t, ()) for t in (4, 10, 14, 15, 5, 11, 16, 17)]
-    for group in (first, second, last):
+    main_run((FIRST, SECOND, LAST))
+
+    @pl.when(jnp.logical_not(helped))
+    def _():
+        rest_run((FIRST, SECOND, LAST))
+
+    @pl.when(core == 0)
+    def _():
+        signal_twin()
+        send_own(1)
+
+    @pl.when(helped)
+    def _():
         for l in range(2):
-            for t, then in group:
-                got(l, t)
-                for s in then:
-                    send(l, s)
-
-    @pl.when(core == 0)
-    def _():
-        pl.semaphore_signal(go_sem, inc=1, device_id=twin, device_id_type=MESH)
-        send_own(1)
+            for t in range(18):
+                given_back(l, t).wait_recv()
 
     for c in mine:
         c.wait()
@@ -283,7 +392,35 @@
         c.wait_send()
     for l in range(2):
         for t in range(18):
-            piece(l, t, plan[t][1:]).wait_send()
+            main_sent(l, t)
+
+    def rest_own_sent(slot):
+        for t in OWN:
+            rest_sent(slot, t)
+
+    @pl.when(jnp.logical_not(helped))
+    def _():
+        rest_own_sent(core)
+        for l in range(2):
+            for t in range(18):
+                if t not in OWN:
+                    rest_sent(l, t)
+
+    @pl.when(jnp.logical_not(early & (core == 1)))
+    def _():
+        rest_own_sent(other)
+
+    @pl.when(early)
+    def _():
+        feed(core).wait_send()
+
+    @pl.when(helps)
+    def _():
+        for l in range(2):
+            for t in range(18):
+                extra_sent(l, t)
+                give_back(l, t).wait_send()
+
     lax.fori_loop(0, MICRO, finish, 0)
 
 
@@ -307,13 +444,15 @@
         out_specs=pl.BlockSpec(memory_space=pl.ANY),
         scratch_shapes=[
             pltpu.VMEM((2, 8, PER, BLOCK, BLOCK), jnp.bfloat16),
+            pltpu.VMEM((2, 8, REST_LEN, BLOCK, BLOCK), jnp.bfloat16),
             pltpu.VMEM((4, MICRO, DB, ROWS, BLOCK), jnp.bfloat16),
             pltpu.VMEM((DB, ROWS, BLOCK), jnp.bfloat16),
             pltpu.VMEM((FB, ROWS, BLOCK), jnp.bfloat16),
             pltpu.VMEM((2, 8, 1, BLOCK), jnp.int32),
             pltpu.SMEM((2, 8, 1, BLOCK), jnp.int32),
             dma((4,)), dma((2,)), dma((2,)), dma((16,)), dma((16,)), dma((1,)),
-            dma((2, 18)), dma((2, 18)), dma((MICRO,)), dma((2, MICRO)),
+            dma((2, 18)), dma((2, 18)), dma((2, 18)), dma((2, 18)), dma((2, 18)), dma((2, 18)),
+            dma((1,)), dma((2,)), dma((2, 18)), dma((2, 18)), dma((MICRO,)), dma((2, MICRO)),
             dma((MICRO, 2)), dma((MICRO, 2)), dma((MICRO, 2)),
             pltpu.SemaphoreType.REGULAR,
         ],

time: 330 us -> 319 us (0.967)
  Pallas kernels: 324 us -> 314 us
    pallas_call x1, Pallas kernels: 324 us -> 314 us  [shards(): pl.pallas_call(relay, out_shape=jax.ShapeDtypeStruct((2, MICRO, 2, DB, 8,...]
where the time goes in v3:
time: 319 us
  Pallas kernels  314 us (98%)
  local copies, waits for them, and re-layouts  3.98 us (1%)
    pallas_call x1, Pallas kernels, shards(): pl.pallas_call(relay, out_shape=jax.ShapeDtypeStruct((2, MICRO, 2, DB, 8,...  314 us

profile of v3, /device:TPU:241, one launch (start us, length us, event | category | flops | bytes accessed | tf_op | source)
XLA Modules:
  0.0 318.9 jit_solution(7983218626572565739)
XLA Ops:
  0.0 0.1 pad.2.clone
  0.1 0.8 reshape.22
  0.8 1.3 add_add_fusion.ids_hbm
  2.2 313.6 %shard_map.55 = bf16[2,8,2,32,8,128]{5,4,3,2,1,0:T(8,128)(2,1)} custom-call(bf16[8,2,32,8,128]{4,3,2,1,0:T(8,128)(2,1)} %bitcast.14, bf16[2,14,128,128]{3,2,1,0:T(8,128)(2,1)} %bitcast.15, bf16[2,32,128,128]{3,2,1,0:T(8,128)(2,1)} %bitcast.13, s32[2,1,128]{2,1,0:T(1,128)} %add_add_fusion.ids_hbm), custom_call_target="tpu_custom_call" | custom-call | tf_op jit(solution)/shard_map/pallas_call | solution.py:440
  315.8 3.1 copy.9
  (1 shorter events, 0.0 us)

commit v4 on v3

--- a/solution.py
+++ b/solution.py
@@ -21,16 +21,19 @@
 LAG = 4
 PIECE = 4
 MAIN = {"A": (0, 17), "A1": (0, 9), "A2": (9, 8), "B": (17, 21), "B1": (17, 11), "B2": (28, 10)}
-REST = {"A": (38, 3), "A1": (38, 2), "A2": (40, 1), "B": (41, 5), "B1": (41, 3), "B2": (44, 2)}
 REST_AT, REST_LEN = 38, 8
 OWN = (0, 6, 12, 1, 7, 13)
 FIRST = ((0, (2, 14)), (6, (8, 15)), (12, (3, 9)), (1, (4,)), (7, (10,)), (13, ()))
 SECOND = ((2, (16,)), (8, (17,)), (3, (5,)), (9, (11,)))
 LAST = tuple((t, ()) for t in (4, 10, 14, 15, 5, 11, 16, 17))
 WAYS = "rrrrrrllllllyyyyyy"
-
-
-def layer(x_ref, y_ref, held_ref, hid_ref, w_ref, ids_ref, emit):
+MAIN_STEPS = (FIRST, SECOND, LAST)
+REST_OWN = (0, 4, 6)
+REST_STEPS = (((0, (1,)), (6, (2, 5)), (4, ())), ((2, (3,)),), ((1, ()), (5, ()), (3, ())))
+REST_WAYS = "rrrrlly"
+
+
+def layer(x_ref, y_ref, held_ref, hid_ref, w_ref, in_ref, out_ref, emit):
     sums = [jnp.zeros((ROWS, BLOCK), jnp.float32) for _ in range(4)]
     for j in range(DB):
         held_ref[j] = x_ref[j]
@@ -43,7 +46,7 @@
         rows, mats = [], []
         for q in (j, j + 1):
             g, b = q // IN_PER, q % IN_PER
-            rows.append(held_ref[ids_ref[g, 0, b]])
+            rows.append(held_ref[in_ref[g, 0, b]])
             mats.append(w_ref[g, b])
         both = jnp.dot(
             jnp.concatenate(rows, axis=0),
@@ -57,7 +60,7 @@
     for step in range(DB + LAG):
         if step < DB:
             g, b = step // OUT_PER, IN_PER + (step % OUT_PER) * K_OUT
-            picked = jnp.concatenate([hid_ref[ids_ref[g, 0, b + k]] for k in range(K_OUT)], axis=1)
+            picked = jnp.concatenate([hid_ref[out_ref[g, step % OUT_PER, k]] for k in range(K_OUT)], axis=1)
             mat = w_ref[g, pl.ds(b, K_OUT)].reshape(K_OUT * BLOCK, BLOCK)
             backs[step] = jnp.dot(picked, mat, preferred_element_type=jnp.float32)
         j = step - LAG
@@ -68,8 +71,8 @@
 
 
 def relay(
-    x_hbm, in_hbm, out_hbm, ids_hbm, res_hbm,
-    w, extra, act, held, hid, ids_vmem, ids_smem,
+    x_hbm, in_hbm, out_hbm, in_ids, out_ids, res_hbm,
+    w, extra, act, held, hid, in_vmem, out_vmem, in_smem, out_smem,
     load_sem, swap_send, swap_recv, ids_send, ids_recv, ids_local,
     ring_send, ring_recv, rest_send, rest_recv, extra_send, extra_recv, feed_send, feed_recv, back_send, back_recv,
     hop_send, hop_recv, res_send, res_recv, res_local, go_sem,
@@ -121,6 +124,13 @@
         ]
         return sends, arrivals
 
+    def rest_plan_of(row):
+        part = (REST_AT, REST_LEN)
+        far = 1 - row
+        sends = [(x, row), (xl, row), (x, far), (xl, far), (x, row), (x, far), (x, row)]
+        arrivals = [(xl, row), (x2, row), (xl, far), (x2, far), (xr, row), (xr, far), (x, far)]
+        return [(at(*p), part) for p in sends], [(at(*p), part) for p in arrivals]
+
     def shard_to(lap, sems):
         return [
             (in_hbm.at[lap], w.at[core, dp, pl.ds(0, IN_PER)]) + tuple(sem.at[0] for sem in sems),
@@ -169,9 +179,8 @@
                 own_copy(lap, WAYS[t], first, count, ring_send.at[slot, t], ring_recv.at[core, t])
 
         def rest():
-            for t in OWN:
-                first, count = REST["A" if t in (0, 6, 13) else "B"]
-                own_copy(lap, WAYS[t], first, count, rest_send.at[slot, t], rest_recv.at[core, t])
+            for t in REST_OWN:
+                own_copy(lap, REST_WAYS[t], REST_AT, REST_LEN, rest_send.at[slot, t], rest_recv.at[core, t])
 
         if lap == 1:
             main()
@@ -193,20 +202,30 @@
 
     for c in mine + swaps:
         c.start()
-    id_own = pltpu.make_async_copy(ids_hbm.at[core], ids_vmem.at[core, dp], ids_local.at[0])
-    id_own.start()
-    id_copies = []
-    for d in range(8):
-        peer = (dp + d) % 8
-        if d:
-            id_copies.append(pltpu.make_async_remote_copy(
-                ids_hbm.at[core], ids_vmem.at[core, dp], ids_send.at[2 * d], ids_recv.at[2 * d],
-                device_id=(section, peer), device_id_type=MESH))
-        id_copies.append(pltpu.make_async_remote_copy(
-            ids_hbm.at[other], ids_vmem.at[core, dp], ids_send.at[2 * d + 1], ids_recv.at[2 * d + 1],
-            device_id=(2 * m + other, peer), device_id_type=MESH))
-    for c in id_copies:
+    tables = ((in_ids, in_vmem), (out_ids, out_vmem))
+
+    def id_copy(n, d, c):
+        source, table = tables[n]
+        return pltpu.make_async_remote_copy(
+            source.at[core if c == 0 else other], table.at[core, dp], ids_send.at[n, 2 * d + c], ids_recv.at[n, 2 * d + c],
+            device_id=(section if c == 0 else 2 * m + other, (dp + d) % 8), device_id_type=MESH)
+
+    def id_landed(n, d, c):
+        source, table = tables[n]
+        return pltpu.make_async_remote_copy(
+            source.at[core], table.at[core if c == 0 else other, (dp + 8 - d) % 8],
+            ids_send.at[n, 2 * d + c], ids_recv.at[n, 2 * d + c],
+            device_id=(section if c == 0 else 2 * m + other, (dp + 8 - d) % 8), device_id_type=MESH)
+
+    id_own = [
+        pltpu.make_async_copy(source.at[core], table.at[core, dp], ids_local.at[n])
+        for n, (source, table) in enumerate(tables)
+    ]
+    id_pairs = [(n, d, c) for n in range(2) for d in range(8) for c in range(2) if d + c > 0]
+    for c in id_own:
         c.start()
+    for key in id_pairs:
+        id_copy(*key).start()
     load_x = [
         pltpu.make_async_copy(x_hbm.at[:, h], act.at[0, :, :, pl.ds(8 * h, 8)], load_sem.at[2 + h]) for h in range(2)
     ]
@@ -216,15 +235,15 @@
         for c in load_x:
             c.start()
 
-    def relay_over(buf, at_block, parts, row, send_sem, recv_sem):
-        sends, arrivals = plan_of(parts, row)
+    def relay_over(buf, at_block, plan, ways, send_sem, recv_sem):
+        sends, arrivals = plan
 
         def piece(l, t, where):
             g, (first, count) = where
             part = buf.at[l, g, pl.ds(first - at_block, count)]
             return pltpu.make_async_remote_copy(
                 part, part, send_sem.at[l, t], recv_sem.at[l, t],
-                device_id=toward(WAYS[t], core), device_id_type=MESH)
+                device_id=toward(ways[t], core), device_id_type=MESH)
 
         def start(l, t):
             piece(l, t, sends[t]).start()
@@ -244,9 +263,10 @@
 
         return start, run, sent, arrivals
 
-    main_start, main_run, main_sent, _ = relay_over(w, 0, MAIN, y, ring_send, ring_recv)
-    rest_start, rest_run, rest_sent, rest_arrivals = relay_over(w, 0, REST, y, rest_send, rest_recv)
-    extra_start, extra_run, extra_sent, extra_arrivals = relay_over(extra, REST_AT, REST, 1 - y, extra_send, extra_recv)
+    main_start, main_run, main_sent, _ = relay_over(w, 0, plan_of(MAIN, y), WAYS, ring_send, ring_recv)
+    rest_start, rest_run, rest_sent, rest_arrivals = relay_over(w, 0, rest_plan_of(y), REST_WAYS, rest_send, rest_recv)
+    extra_start, extra_run, extra_sent, extra_arrivals = relay_over(
+        extra, REST_AT, rest_plan_of(1 - y), REST_WAYS, extra_send, extra_recv)
 
     def give_back(l, t):
         g, (first, count) = extra_arrivals[t]
@@ -273,9 +293,9 @@
     def _():
         for l in range(2):
             fed(l).wait_recv()
-            for t in OWN:
+            for t in REST_OWN:
                 extra_start(l, t)
-        extra_run((FIRST, SECOND, LAST), lambda l, t: give_back(l, t).start())
+        extra_run(REST_STEPS, lambda l, t: give_back(l, t).start())
         signal_twin()
         send_own(0)
 
@@ -289,11 +309,11 @@
         pl.semaphore_wait(go_sem, 1)
         send_own(1)
 
-    main_run((FIRST, SECOND, LAST))
+    main_run(MAIN_STEPS)
 
     @pl.when(jnp.logical_not(helped))
     def _():
-        rest_run((FIRST, SECOND, LAST))
+        rest_run(REST_STEPS)
 
     @pl.when(core == 0)
     def _():
@@ -303,28 +323,25 @@
     @pl.when(helped)
     def _():
         for l in range(2):
-            for t in range(18):
+            for t in range(7):
                 given_back(l, t).wait_recv()
 
     for c in mine:
         c.wait()
     for c in landed:
         c.wait_recv()
-    id_own.wait()
-    for d in range(8):
-        back = (dp + 8 - d) % 8
-        if d:
-            pltpu.make_async_remote_copy(
-                ids_hbm.at[core], ids_vmem.at[core, back], ids_send.at[2 * d], ids_recv.at[2 * d],
-                device_id=(section, back), device_id_type=MESH).wait_recv()
-        pltpu.make_async_remote_copy(
-            ids_hbm.at[core], ids_vmem.at[other, back], ids_send.at[2 * d + 1], ids_recv.at[2 * d + 1],
-            device_id=(2 * m + other, back), device_id_type=MESH).wait_recv()
-    for c in id_copies:
-        c.wait_send()
-    fetch = pltpu.make_async_copy(ids_vmem, ids_smem, ids_local.at[0])
-    fetch.start()
-    fetch.wait()
+    for c in id_own:
+        c.wait()
+    for key in id_pairs:
+        id_landed(*key).wait_recv()
+    fetch = [
+        pltpu.make_async_copy(in_vmem, in_smem, ids_local.at[0]),
+        pltpu.make_async_copy(out_vmem, out_smem, ids_local.at[1]),
+    ]
+    for c in fetch:
+        c.start()
+    for c in fetch:
+        c.wait()
 
     @pl.when(stage == 0)
     def _():
@@ -366,8 +383,8 @@
         def _():
             hop(i, 0).wait_recv()
 
-        layer(act.at[0, i], act.at[1, i], held, hid, w.at[0], ids_smem.at[0], None)
-        layer(act.at[1, i], act.at[2, i], held, hid, w.at[1], ids_smem.at[1], functools.partial(send_hop, i))
+        layer(act.at[0, i], act.at[1, i], held, hid, w.at[0], in_smem.at[0], out_smem.at[0], None)
+        layer(act.at[1, i], act.at[2, i], held, hid, w.at[1], in_smem.at[1], out_smem.at[1], functools.partial(send_hop, i))
         for h in range(2):
             result_local(i, h).start()
             result_remote(i, h).start()
@@ -390,21 +407,22 @@
 
     for c in swaps:
         c.wait_send()
+    for key in id_pairs:
+        id_copy(*key).wait_send()
     for l in range(2):
         for t in range(18):
             main_sent(l, t)
 
     def rest_own_sent(slot):
-        for t in OWN:
+        for t in REST_OWN:
             rest_sent(slot, t)
 
     @pl.when(jnp.logical_not(helped))
     def _():
         rest_own_sent(core)
         for l in range(2):
-            for t in range(18):
-                if t not in OWN:
-                    rest_sent(l, t)
+            for t in (1, 2, 3, 5):
+                rest_sent(l, t)
 
     @pl.when(jnp.logical_not(early & (core == 1)))
     def _():
@@ -417,7 +435,7 @@
     @pl.when(helps)
     def _():
         for l in range(2):
-            for t in range(18):
+            for t in range(7):
                 extra_sent(l, t)
                 give_back(l, t).wait_send()
 
@@ -428,19 +446,11 @@
     x = inputs.reshape(MICRO, 2, 8, DB, BLOCK).transpose(0, 1, 3, 2, 4)
     w_in = in_blocks.reshape(2, IN_PER, BLOCK, BLOCK)
     w_out = out_blocks.reshape(2, OUT_PER * K_OUT, BLOCK, BLOCK)
-    ids = jnp.concatenate(
-        [
-            in_ids.reshape(2, 1, IN_PER),
-            out_ids.reshape(2, 1, OUT_PER * K_OUT),
-            jnp.zeros((2, 1, BLOCK - PER), jnp.int32),
-        ],
-        axis=2,
-    )
     dma = pltpu.SemaphoreType.DMA
     result = pl.pallas_call(
         relay,
         out_shape=jax.ShapeDtypeStruct((2, MICRO, 2, DB, 8, BLOCK), jnp.bfloat16),
-        in_specs=[pl.BlockSpec(memory_space=pl.ANY)] * 4,
+        in_specs=[pl.BlockSpec(memory_space=pl.ANY)] * 5,
         out_specs=pl.BlockSpec(memory_space=pl.ANY),
         scratch_shapes=[
             pltpu.VMEM((2, 8, PER, BLOCK, BLOCK), jnp.bfloat16),
@@ -448,18 +458,20 @@
             pltpu.VMEM((4, MICRO, DB, ROWS, BLOCK), jnp.bfloat16),
             pltpu.VMEM((DB, ROWS, BLOCK), jnp.bfloat16),
             pltpu.VMEM((FB, ROWS, BLOCK), jnp.bfloat16),
-            pltpu.VMEM((2, 8, 1, BLOCK), jnp.int32),
-            pltpu.SMEM((2, 8, 1, BLOCK), jnp.int32),
-            dma((4,)), dma((2,)), dma((2,)), dma((16,)), dma((16,)), dma((1,)),
-            dma((2, 18)), dma((2, 18)), dma((2, 18)), dma((2, 18)), dma((2, 18)), dma((2, 18)),
-            dma((1,)), dma((2,)), dma((2, 18)), dma((2, 18)), dma((MICRO,)), dma((2, MICRO)),
+            pltpu.VMEM((2, 8, 1, IN_PER), jnp.int32),
+            pltpu.VMEM((2, 8, OUT_PER, K_OUT), jnp.int32),
+            pltpu.SMEM((2, 8, 1, IN_PER), jnp.int32),
+            pltpu.SMEM((2, 8, OUT_PER, K_OUT), jnp.int32),
+            dma((4,)), dma((2,)), dma((2,)), dma((2, 16)), dma((2, 16)), dma((2,)),
+            dma((2, 18)), dma((2, 18)), dma((2, 7)), dma((2, 7)), dma((2, 7)), dma((2, 7)),
+            dma((1,)), dma((2,)), dma((2, 7)), dma((2, 7)), dma((MICRO,)), dma((2, MICRO)),
             dma((MICRO, 2)), dma((MICRO, 2)), dma((MICRO, 2)),
             pltpu.SemaphoreType.REGULAR,
         ],
         compiler_params=pltpu.CompilerParams(
             collective_id=0, has_side_effects=True, vmem_limit_bytes=60 * 2**20
         ),
-    )(x, w_in, w_out, ids)
+    )(x, w_in, w_out, in_ids.reshape(2, 1, IN_PER), out_ids.reshape(2, OUT_PER, K_OUT))
     result = result.transpose(0, 1, 2, 4, 3, 5).reshape(2, 1, MICRO, ROWS, DB * BLOCK)
     return result
 

time: 319 us -> 318 us (level)
  no operation moved by 1% of the time
where the time goes in v4:
time: 318 us; the launch traced here: 317 us
  Pallas kernels  314 us (99%)
    pallas_call x1, Pallas kernels, shards(): pl.pallas_call(relay, out_shape=jax.ShapeDtypeStruct((2, MICRO, 2, DB, 8,...  314 us

profile of v4, /device:TPU:241, one launch (start us, length us, event | category | flops | bytes accessed | tf_op | source)
XLA Modules:
  0.0 317.3 jit_solution(2118085364271587313)
XLA Ops:
  0.0 314.2 %shard_map.55 = bf16[2,8,2,32,8,128]{5,4,3,2,1,0:T(8,128)(2,1)} custom-call(bf16[8,2,32,8,128]{4,3,2,1,0:T(8,128)(2,1)} %bitcast.14, bf16[2,14,128,128]{3,2,1,0:T(8,128)(2,1)} %bitcast.15, bf16[2,32,128,128]{3,2,1,0:T(8,128)(2,1)} %bitcast.13, s32[2,1,14]{2,1,0:T(1,128)} %bitcast.17, s32[2,4,8]{2,1,0:T(4,128)} %bitcast.16), custom_call_target="tpu_custom_call" | custom-call | tf_op jit(solution)/shard_map/pallas_call | solution.py:450
  314.2 3.1 copy.8
